TPU v7x, 32 devices: a whole 2x2x4 slice. The times are simulated.
32 devices in a mesh: seq: 16 (over z, x, core), head: 2 (over y).
Axes of the slice: x: 2, y: 2, z: 4, core: 2. Of those that a mesh axis runs over, the one named last changes fastest.
Arguments:
- queries: bfloat16 [16384, 2048], P(('seq', 'head')), may hold values from -6 to 6
- key_rows: bfloat16 [16384, 2048], P(('seq', 'head')), may hold values from -6 to 6
- values: bfloat16 [16384, 4096], P(('seq', 'head')), may hold values from -140 to 140
- in_gate: bfloat16 [16384, 8], P(('seq', 'head')), may hold values from -6 to 226
- forget_gate: bfloat16 [16384, 8], P(('seq', 'head')), may hold values from -0.25 to 15
- out_gate: bfloat16 [16384, 4096], P(('seq', 'head')), may hold values from -6 to 6
- norm_gain: float32 [4096], P('head'), may hold values from 0.1 to 1.9
Outputs:
- layer_out: bfloat16 [16384, 4096], P(('seq', 'head'))
All inputs are finite; a program needn't handle non-finite values.
Results may differ from a plain program's by a relative error of at most 0.0085.
Values may be sent and summed in bfloat16 or wider, within the bound.
A program may use at most 192 MiB of HBM per device.

v0:
```python
import jax
import jax.numpy as jnp
from jax import lax
from jax.sharding import PartitionSpec as P

STRETCH = 1024
far_below = -1e30
norm_eps = 1e-06


def prefix_2(part, axis, combine, identity):
    place = lax.axis_index(axis)
    gathered = jax.tree.map(lambda a: lax.all_gather(a, axis), part)
    state = jax.tree.map(lambda a, e: jnp.zeros_like(a) + jnp.asarray(e, a.dtype), part, identity)

    def one(step, state):
        return combine(
            state, jax.tree.map(lambda a: lax.dynamic_index_in_dim(a, step, 0, False), gathered)
        )

    return lax.fori_loop(0, place, one, state)


def combine(earlier, later):
    state_a, max_a, decay_a = earlier
    state_b, max_b, decay_b = later
    shifted = max_a + decay_b
    joint_max = jnp.maximum(shifted, max_b)
    state_total_sum = (
        jnp.exp(shifted - joint_max)[..., None, None] * state_a
        + jnp.exp(max_b - joint_max)[..., None, None] * state_b
    )
    return (state_total_sum, joint_max, decay_a + decay_b)


def summarize(keys_blk, values_block, in_blk, forget_blk):
    log_forget = jax.nn.log_sigmoid(forget_blk.astype(jnp.float32))
    running = jnp.cumsum(log_forget, axis=0)
    final_cum = running[-1]
    log_weight = final_cum[None, :] - running + in_blk.astype(jnp.float32)
    block_max = jnp.max(log_weight, axis=0)
    weighted_values = (
        jnp.exp(log_weight - block_max[None, :])[:, :, None] * keys_blk.astype(jnp.float32)
    ).astype(jnp.bfloat16)
    state_total_sum = jnp.einsum(
        "yij,yip->ijp", weighted_values, values_block, preferred_element_type=jnp.float32
    )
    return (running, (state_total_sum, block_max, final_cum))


def block_output(query_block, keys_blk, values_block, in_blk, running, prefix):
    prefix_state = prefix[0]
    prefix_max = prefix[1]
    scores = jnp.einsum("thk,shk->hts", query_block, keys_blk, preferred_element_type=jnp.float32)
    cum_rows = running.T
    input_rows = in_blk.astype(jnp.float32).T
    log_weight = cum_rows[:, :, None] - cum_rows[:, None, :] + input_rows[:, None, :]
    span_rows = running.shape[0]
    causal = lax.broadcasted_iota(jnp.int32, (span_rows, span_rows), 0) >= lax.broadcasted_iota(
        jnp.int32, (span_rows, span_rows), 1
    )
    log_weight = jnp.where(causal[None], log_weight, -jnp.inf)
    carried = cum_rows + prefix_max[:, None]
    row_max = jnp.maximum(carried, jnp.max(log_weight, axis=2))
    mixed_weights = (scores * jnp.exp(log_weight - row_max[:, :, None])).astype(jnp.bfloat16)
    within = jnp.einsum(
        "hts,shv->thv", mixed_weights, values_block, preferred_element_type=jnp.float32
    )
    preceding_portion = jnp.einsum(
        "ydw,dwl->ydl",
        query_block,
        prefix_state.astype(jnp.bfloat16),
        preferred_element_type=jnp.float32,
    )
    return within + jnp.exp(carried - row_max).T[:, :, None] * preceding_portion


def local(queries, key_rows, values, in_gate, forget_gate, out_gate, norm_gain):
    moved = (
        lax.all_to_all(queries, "head", split_axis=1, concat_axis=0, tiled=True),
        lax.all_to_all(key_rows, "head", split_axis=1, concat_axis=0, tiled=True),
        lax.all_to_all(values, "head", split_axis=1, concat_axis=0, tiled=True),
        lax.all_to_all(in_gate, "head", split_axis=1, concat_axis=0, tiled=True),
        lax.all_to_all(forget_gate, "head", split_axis=1, concat_axis=0, tiled=True),
        lax.all_to_all(out_gate, "head", split_axis=1, concat_axis=0, tiled=True),
    )
    gate_rows = moved[5]
    heads_here = moved[3].shape[1]
    total_rows = moved[0].shape[0]
    key_width = moved[0].shape[1] // heads_here
    value_width = moved[2].shape[1] // heads_here
    blocks = total_rows // STRETCH
    query_all = moved[0].reshape(blocks, STRETCH, heads_here, key_width)
    keys_all = moved[1].reshape(blocks, STRETCH, heads_here, key_width)
    values_all = moved[2].reshape(blocks, STRETCH, heads_here, value_width)
    input_all = moved[3].reshape(blocks, STRETCH, heads_here)
    forget_all = moved[4].reshape(blocks, STRETCH, heads_here)
    index_blk = 0
    running, summary = summarize(
        keys_all[index_blk], values_all[index_blk], input_all[index_blk], forget_all[index_blk]
    )
    running_list = [running]
    identity = (
        jnp.zeros((heads_here, key_width, value_width), jnp.float32),
        jnp.full((heads_here,), far_below, jnp.float32),
        jnp.zeros((heads_here,), jnp.float32),
    )
    prefix = prefix_2(summary, "seq", combine, identity)
    index_blk = 0
    mixed_blk = block_output(
        query_all[index_blk],
        keys_all[index_blk],
        values_all[index_blk],
        input_all[index_blk],
        running_list[index_blk],
        prefix,
    )
    mean_sq = jnp.mean(mixed_blk * mixed_blk, axis=-1, keepdims=True)
    normed = (
        mixed_blk * lax.rsqrt(mean_sq + norm_eps) * norm_gain.reshape(heads_here, value_width)
    ).astype(jnp.bfloat16)
    normed = normed.reshape(total_rows, heads_here * value_width)
    gated = (jax.nn.sigmoid(gate_rows.astype(jnp.float32)) * normed.astype(jnp.float32)).astype(
        jnp.bfloat16
    )
    return lax.all_to_all(gated, "head", split_axis=0, concat_axis=1, tiled=True)


def solution(mesh):
    placed = (
        P(("seq", "head"), None),
        P(("seq", "head"), None),
        P(("seq", "head"), None),
        P(("seq", "head"), None),
        P(("seq", "head"), None),
        P(("seq", "head"), None),
        P("head"),
    )
    return jax.shard_map(
        local, mesh=mesh, in_specs=placed, out_specs=P(("seq", "head"), None), check_vma=False
    )
```

profile of v0, /device:TPU:27, one launch (start us, length us, event | category | flops | bytes accessed | tf_op | source)
XLA Modules:
  0.0 439.4 jit_solution(12269905239405438814)
XLA Ops:
  7.8 3.2 all-to-all-start.3
  13.7 3.2 all-to-all-start.4
  17.0 2.9 copy.53
  22.3 3.8 all-to-all-start.2
  26.1 4.8 %copy.100 = bf16[64,2,8,2048]{3,2,0,1:T(8,128)(2,1)} copy(bf16[64,2,8,2048]{3,2,1,0:T(8,128)(2,1)} %bitcast.114) | data formatting | bytes 8388608 | tf_op jit(solution)/shard_map/all_to_all | solution.py:82
  30.9 18.3 %all-to-all-done.2 = bf16[512,2,1024]{2,0,1:T(8,128)(2,1)S(1)} async-done(((bf16[512,2,1024]{2,0,1:T(8,128)(2,1)}), bf16[512,2,1024]{2,0,1:T(8,128)(2,1)S(1)}, u32[]{:S(2)}, u32[]{:S(2)}) %all-to-all-start.2) | async-done | bytes 2097184 | tf_op jit(solution)/shard_map/all_to_all | solution.py:81
  50.5 5.6 %all-to-all-start.5 = ((bf16[512,2,2048]{2,0,1:T(8,128)(2,1)}), bf16[512,2,2048]{2,0,1:T(8,128)(2,1)}, u32[]{:S(2)}, u32[]{:S(2)}) async-start(bf16[512,2,2048]{2,0,1:T(8,128)(2,1)} %bitcast.106), calls=%async_computation.5 | async-start | bytes 8388608 | tf_op jit(solution)/shard_map/all_to_all | solution.py:82
  58.5 3.3 squeeze_reshape.12
  64.1 36.8 %all-to-all-done.5 = bf16[512,2,2048]{2,0,1:T(8,128)(2,1)} async-done(((bf16[512,2,2048]{2,0,1:T(8,128)(2,1)}), bf16[512,2,2048]{2,0,1:T(8,128)(2,1)}, u32[]{:S(2)}, u32[]{:S(2)}) %all-to-all-start.5) | async-done | bytes 4194336 | tf_op jit(solution)/shard_map/all_to_all | solution.py:82
  100.9 7.8 %squeeze_reshape.13 = bf16[1024,4,512]{2,1,0:T(4,128)(2,1)} reshape(bf16[2,512,2048]{2,1,0:T(8,128)(2,1)} %bitcast.20) | data formatting | bytes 8388608 | tf_op jit(solution)/shard_map/squeeze;reshape | solution.py:113
  108.7 7.5 %copy.65 = bf16[1024,4,512]{0,2,1:T(8,128)(2,1)} copy(bf16[1024,4,512]{2,1,0:T(4,128)(2,1)} %squeeze_reshape.13) | data formatting | bytes 8388608 | tf_op jit(solution)/shard_map/squeeze;reshape | solution.py:113
  116.2 5.7 %fusion.9 = f32[4,256,512]{2,1,0:T(8,128)} fusion(bf16[1024,4,512]{0,2,1:T(8,128)(2,1)} %copy.65, bf16[1024,4,256]{2,1,0:T(4,128)(2,1)} %multiply_convert_fusion.2), kind=kOutput, calls=%fused_computation.24 | convolution fusion | flops 1073741824 | bytes 8388608 | tf_op jit(solution)/shard_map/yij,yip->ijp/dot_general | solution.py:45
  123.5 3.8 all-to-all-start.1
  127.4 6.6 %copy.51 = bf16[512,4096]{0,1:T(8,128)(2,1)} copy(bf16[512,4096]{1,0:T(8,128)(2,1)} %param.14) | data formatting | bytes 8388608 | tf_op args[5]
  136.7 30.6 %all-reduce = f32[64]{0:T(128)S(1)} all-reduce(f32[64]{0:T(128)S(1)} %dynamic-update-slice), channel_id=2, replica_groups=mesh['seq'=16,'head'=2] {'seq'}, use_global_device_ids=true, to_apply=%add | all-reduce | flops 64 | bytes 512
  167.6 20.2 %all-gather.2 = f32[16,1,4]{2,1,0:T(1,128)S(1)} all-gather(f32[1,1,4]{2,1,0:T(1,128)S(1)} %get-tuple-element.111), channel_id=1, replica_groups=mesh['seq'=16,'head'=2] {'seq'}, dimensions={0}, use_global_device_ids=true | all-gather | bytes 272 | tf_op jit(solution)/shard_map/all_gather | solution.py:13
  187.8 5.2 %fusion.5 = f32[4,1024]{1,0:T(4,128)S(1)} fusion(f32[4,1024]{1,0:T(4,128)S(1)} %copy.58, f32[4,1024]{1,0:T(4,128)S(1)} %bitcast.118, pred[1024,1024]{1,0:T(8,128)(4,1)} %iota_compare_fusion), kind=kLoop, calls=%fused_computation.12 | loop fusion | flops 16773120 | bytes 1097728 | tf_op jit(solution)/shard_map/reduce_max | solution.py:64
  193.0 5.8 %all-to-all-start = ((bf16[512,2,2048]{0,2,1:T(8,128)(2,1)}), bf16[512,2,2048]{0,2,1:T(8,128)(2,1)}, u32[]{:S(2)}, u32[]{:S(2)}) async-start(bf16[512,2,2048]{0,2,1:T(8,128)(2,1)} %bitcast.105), calls=%async_computation | async-start | bytes 8388608 | tf_op jit(solution)/shard_map/all_to_all | solution.py:85
  198.8 2.7 squeeze_reshape.11
  201.5 91.4 %all-gather.5.cloned.1.call-done = f32[64,256,512]{2,1,0:T(8,128)} async-done(((f32[4,256,512]{2,1,0:T(8,128)}), f32[64,256,512]{2,1,0:T(8,128)}) %all-gather.5.cloned.1.call-update) | async-done | bytes 33554448 | tf_op jit(solution)/shard_map/all_gather | solution.py:13
  293.2 39.9 %while.14 = (s32[]{:T(128)}, f32[4,256,512]{2,1,0:T(8,128)S(1)}, f32[4]{0:T(128)S(1)}, s32[]{:T(128)}, f32[16,4]{1,0:T(8,128)S(1)}, /*index=5*/f32[16,4]{1,0:T(8...) while((s32[]{:T(128)}, f32[4,256,512]{2,1,0:T(8,128)S(1)}, f32[4]{0:T(128)S(1)}, ...), condition=%wide.region_4.5_spmd, body=%wide.region_3.4_spmd.sunk | while | flops 1572885 | bytes 6291763 | solution.py:21
  293.3 2.6 fusion.27
  296.0 2.6 fusion.27
  322.5 2.6 fusion.27
  327.7 2.6 fusion.27
  333.3 14.9 %fusion.13 = f32[4,1024,512]{1,2,0:T(8,128)} fusion(bf16[1024,4,512]{0,2,1:T(8,128)(2,1)} %copy.65, f32[4,1024]{1,0:T(4,128)S(1)} %get-tuple-element.113, f32[4,1024]{1,0:T(4,128)S(1)} %copy.58, f32[4,1024]{1,0:T(4,128)S(1)} %bitcast.119, pred[1024,1024]{1,0:T(8,128)(4,1)S(1)} %copy-done.2, bf16[1024,4,256]{2,1,0:T(4,128)(2,1)} %copy-done, ...), kind=kOutput, calls=%fused_computation.27 | convolution fusion | flops 6467616768 | bytes 17874944 | tf_op jit(solution)/shard_map/hts,shv->thv/dot_general | solution.py:66
  348.2 6.2 %multiply_reduce_fusion = (f32[1024,4]{0,1:T(4,128)S(1)}, f32[1024,4,512]{0,2,1:T(8,128)S(1)}) fusion(bf16[1024,4,256]{2,1,0:T(4,128)(2,1)} %squeeze_reshape.11, f32[4,256,512]{2,1,0:T(8,128)S(1)} %get-tuple-element.65, f32[1024,4]{0,1:T(4,128)S(1)} %get-tuple-element.112, f32[4,1024,512]{1,2,0:T(8,128)} %fusion.13), kind=kOutput, calls=%fused_computation.18 | convolution fusion | flops 1082650624 | bytes 21004288 | tf_op jit(solution)/shard_map/ydw,dwl->ydl/dot_general | solution.py:69
  354.4 4.0 fusion.8
  358.4 11.8 %reshape.113 = f32[2,512,2048]{1,0,2:T(2,128)} reshape(f32[1024,4,512]{0,2,1:T(8,128)} %fusion.8) | data formatting | bytes 16777216 | tf_op jit(solution)/shard_map/convert_element_type | solution.py:123
  370.2 6.7 %fusion.7 = bf16[2,512,2048]{1,2,0:T(8,128)(2,1)S(1)} fusion(f32[2,512,2048]{1,0,2:T(2,128)} %reshape.113, bf16[512,2,2048]{0,2,1:T(8,128)(2,1)} %all-to-all-done), kind=kLoop, calls=%fused_computation.16 | loop fusion | flops 12582912 | bytes 16777216 | tf_op jit(solution)/shard_map/convert_element_type | solution.py:123
  376.8 49.4 %all_to_all.103 = bf16[2,512,2048]{1,2,0:T(8,128)(2,1)} all-to-all(bf16[2,512,2048]{1,2,0:T(8,128)(2,1)S(1)} %fusion.7), channel_id=1, replica_groups=mesh['seq'=16,'head'=2] {'head'}, dimensions={0} | all-to-all | bytes 8388608 | tf_op jit(solution)/shard_map/all_to_all | solution.py:126
  426.2 6.3 %copy.69 = bf16[512,4096]{1,0:T(8,128)(2,1)} copy(bf16[512,4096]{0,1:T(8,128)(2,1)} %bitcast.107) | data formatting | bytes 8388608 | tf_op jit(solution)/shard_map/all_to_all | solution.py:126
  (89 shorter events, 45.5 us)
Async XLA Ops:
  7.8 5.9 %all-to-all-start.3 = ((bf16[512,2,4]{0,2,1:T(4,128)(2,1)}), bf16[512,2,4]{0,2,1:T(4,128)(2,1)S(1)}, u32[]{:S(2)}, u32[]{:S(2)}) async-start(bf16[512,2,4]{0,2,1:T(4,128)(2,1)} %all_to_all.86), calls=%async_computation.3 | async-start | bytes 16384 | tf_op jit(solution)/shard_map/all_to_all | solution.py:84
  13.7 8.6 %all-to-all-start.4 = ((bf16[512,2,4]{0,2,1:T(4,128)(2,1)}), bf16[512,2,4]{0,2,1:T(4,128)(2,1)S(1)}, u32[]{:S(2)}, u32[]{:S(2)}) async-start(bf16[512,2,4]{0,2,1:T(4,128)(2,1)} %all_to_all.88), calls=%async_computation.4 | async-start | bytes 16384 | tf_op jit(solution)/shard_map/all_to_all | solution.py:83
  22.3 26.9 %all-to-all-start.2 = ((bf16[512,2,1024]{2,0,1:T(8,128)(2,1)}), bf16[512,2,1024]{2,0,1:T(8,128)(2,1)S(1)}, u32[]{:S(2)}, u32[]{:S(2)}) async-start(bf16[512,2,1024]{2,0,1:T(8,128)(2,1)} %copy.54), calls=%async_computation.2 | async-start | bytes 4194304 | tf_op jit(solution)/shard_map/all_to_all | solution.py:81
  49.2 1.3 copy-start.1
  50.5 50.4 %all-to-all-start.5 = ((bf16[512,2,2048]{2,0,1:T(8,128)(2,1)}), bf16[512,2,2048]{2,0,1:T(8,128)(2,1)}, u32[]{:S(2)}, u32[]{:S(2)}) async-start(bf16[512,2,2048]{2,0,1:T(8,128)(2,1)} %bitcast.106), calls=%async_computation.5 | async-start | bytes 8388608 | tf_op jit(solution)/shard_map/all_to_all | solution.py:82
  56.1 236.8 %all-gather.5.cloned.1.call-start = ((), (), s32[]{:S(2)}) async-start(), calls=%async_computation.7 | async-start | bytes 35651584 | tf_op jit(solution)/shard_map/all_gather | solution.py:13
  61.9 46.9 %copy-start = (bf16[1024,4,256]{2,1,0:T(4,128)(2,1)}, bf16[1024,4,256]{2,1,0:T(4,128)(2,1)S(1)}, u32[]{:S(2)}) copy-start(bf16[1024,4,256]{2,1,0:T(4,128)(2,1)S(1)} %squeeze_reshape.12) | copy-start | bytes 6291460
  116.2 5.8 %copy-start.3 = (bf16[512,2048]{1,0:T(8,128)(2,1)S(1)}, bf16[512,2048]{1,0:T(8,128)(2,1)}, u32[]{:S(2)}) copy-start(bf16[512,2048]{1,0:T(8,128)(2,1)} %param.9) | copy-start | bytes 6291460
  122.0 5.3 %copy-start.4 = (f32[2048]{0:T(1024)S(1)}, f32[2048]{0:T(1024)}, u32[]{:S(2)}) copy-start(f32[2048]{0:T(1024)} %param.15) | copy-start | bytes 24580
  123.5 69.4 %all-to-all-start.1 = ((bf16[512,2,1024]{2,0,1:T(8,128)(2,1)}), bf16[512,2,1024]{2,0,1:T(8,128)(2,1)S(1)}, u32[]{:S(2)}, u32[]{:S(2)}) async-start(bf16[512,2,1024]{2,0,1:T(8,128)(2,1)} %bitcast.110), calls=%async_computation.1 | async-start | bytes 4194304 | tf_op jit(solution)/shard_map/all_to_all | solution.py:80
  127.3 6.6 %copy-start.5 = (u32[32]{0:T(128)S(1)}, u32[32]{0:T(128)}, u32[]{:S(2)}) copy-start(u32[32]{0:T(128)} %constant.48) | copy-start | bytes 388
  193.0 177.2 %all-to-all-start = ((bf16[512,2,2048]{0,2,1:T(8,128)(2,1)}), bf16[512,2,2048]{0,2,1:T(8,128)(2,1)}, u32[]{:S(2)}, u32[]{:S(2)}) async-start(bf16[512,2,2048]{0,2,1:T(8,128)(2,1)} %bitcast.105), calls=%async_computation | async-start | bytes 8388608 | tf_op jit(solution)/shard_map/all_to_all | solution.py:85
  293.2 40.1 %copy-start.2 = (pred[1024,1024]{1,0:T(8,128)(4,1)S(1)}, pred[1024,1024]{1,0:T(8,128)(4,1)}, u32[]{:S(2)}) copy-start(pred[1024,1024]{1,0:T(8,128)(4,1)} %iota_compare_fusion) | copy-start | bytes 3145732
Sparse Core Ops, SparseCore 0:
  122.1 170.7 all-gather.4
where the time goes:
time: 441 us; the launch traced here: 439 us
  waiting for transfers between devices  148 us (34%)
  blocking collectives  100 us (23%)
  local copies, waits for them, and re-layouts  63.7 us (14%)
  other arithmetic  60.4 us (14%)
  matrix products  26.8 us (6%)
  starting transfers between devices  25.4 us (6%)
  between operations  14.3 us (3%)
    all_gather x1, waiting for transfers between devices, prefix_2(): gathered = jax.tree.map(lambda a: lax.all_gather(a, axis), part)  91.4 us
    all_to_all x1, blocking collectives, local(): lax.all_to_all(gated, 'head', split_axis=0, concat_axis=1, tiled=True)  49.4 us
    add x15, other arithmetic, combine(): jnp.exp(shifted - joint_max)[..., None, None] * state_a  38.7 us
    all_to_all x1, waiting for transfers between devices, local(): lax.all_to_all(values, 'head', split_axis=1, concat_axis=0, tiled=True)  36.8 us
    unnamed x1, blocking collectives  30.6 us
    all_gather x1, blocking collectives, prefix_2(): gathered = jax.tree.map(lambda a: lax.all_gather(a, axis), part)  20.2 us
    all_to_all x1, waiting for transfers between devices, local(): lax.all_to_all(key_rows, 'head', split_axis=1, concat_axis=0, tiled=True)  18.3 us
    another operation x2, local copies, waits for them, and re-layouts, local(): values_all[index_blk]  15.3 us
  transfers between devices with their start and end apart: 7, of which 4 were waited for; matrix products, arithmetic and copies ran while one was open for 26% of the time, Pallas kernels for 0%

commit v1 on v0

--- a/solution.py
+++ b/solution.py
@@ -123,7 +123,10 @@
     gated = (jax.nn.sigmoid(gate_rows.astype(jnp.float32)) * normed.astype(jnp.float32)).astype(
         jnp.bfloat16
     )
-    return lax.all_to_all(gated, "head", split_axis=0, concat_axis=1, tiled=True)
+    return jnp.concatenate(
+        lax.all_to_all(jnp.stack(jnp.split(gated, lax.axis_size("head"), axis=0)), "head", 0, 0),
+        axis=1,
+    )
 
 
 def solution(mesh):

time: 441 us -> 426 us (0.966)
  waiting for transfers between devices: 148 us -> 125 us
    all_gather x1, waiting for transfers between devices: 91.4 us -> 59.6 us  [prefix_2(): gathered = jax.tree.map(lambda a: lax.all_gather(a, axis), part)]
    convert_element_type x1 -> x0, local copies, waits for them, and re-layouts: 11.8 us -> none  [local(): normed.astype(jnp.float32)]
    div x0 -> x1, local copies, waits for them, and re-layouts: none -> 9.32 us  [local(): jax.nn.sigmoid(gate_rows.astype(jnp.float32)) * normed.astype(jnp.float32)]
    all_to_all x1, waiting for transfers between devices: 0.01 us -> 8.56 us  [local(): lax.all_to_all(queries, 'head', split_axis=1, concat_axis=0, tiled=True)]
    div x0 -> x1, other arithmetic: none -> 7.63 us  [local(): jax.nn.sigmoid(gate_rows.astype(jnp.float32)) * normed.astype(jnp.float32)]
    reshape x0 -> x1, local copies, waits for them, and re-layouts: none -> 6.32 us  [local(): jnp.concatenate(lax.all_to_all(jnp.stack(jnp.split(gated, lax.axis_size('...]
  transfers between devices with their start and end apart: 7 -> 7, of which waited for: 4 -> 5; matrix products, arithmetic and copies ran while one was open for 26% -> 14% of each run, Pallas kernels for 0% -> 0%
where the time goes in v1:
time: 426 us; the launch traced here: 424 us
  waiting for transfers between devices  125 us (29%)
  blocking collectives  100 us (23%)
  local copies, waits for them, and re-layouts  67.9 us (16%)
  other arithmetic  63.5 us (15%)
  matrix products  26.8 us (6%)
  starting transfers between devices  25.3 us (6%)
  between operations  14.3 us (3%)
    all_gather x1, waiting for transfers between devices, prefix_2(): gathered = jax.tree.map(lambda a: lax.all_gather(a, axis), part)  59.6 us
    all_to_all x1, blocking collectives, local(): lax.all_to_all(jnp.stack(jnp.split(gated, lax.axis_size('head'), axis=0))...  49.4 us
    add x15, other arithmetic, combine(): jnp.exp(shifted - joint_max)[..., None, None] * state_a  38.7 us
    all_to_all x1, waiting for transfers between devices, local(): lax.all_to_all(values, 'head', split_axis=1, concat_axis=0, tiled=True)  36.8 us
    unnamed x1, blocking collectives  30.6 us
    all_gather x1, blocking collectives, prefix_2(): gathered = jax.tree.map(lambda a: lax.all_gather(a, axis), part)  20.4 us
    all_to_all x1, waiting for transfers between devices, local(): lax.all_to_all(key_rows, 'head', split_axis=1, concat_axis=0, tiled=True)  18.3 us
    another operation x2, local copies, waits for them, and re-layouts, local(): values_all[index_blk]  15.3 us
  transfers between devices with their start and end apart: 7, of which 5 were waited for; matrix products, arithmetic and copies ran while one was open for 14% of the time, Pallas kernels for 0%

profile of v1, /device:TPU:27, one launch (start us, length us, event | category | flops | bytes accessed | tf_op | source)
XLA Modules:
  0.0 423.5 jit_solution(12279987506252182197)
XLA Ops:
  7.8 3.2 all-to-all-start.3
  13.7 3.2 all-to-all-start.4
  16.9 2.9 copy.53
  22.3 3.8 all-to-all-start.2
  26.1 4.8 %copy.100 = bf16[64,2,8,2048]{3,2,0,1:T(8,128)(2,1)} copy(bf16[64,2,8,2048]{3,2,1,0:T(8,128)(2,1)} %bitcast.119) | data formatting | bytes 8388608 | tf_op jit(solution)/shard_map/all_to_all | solution.py:82
  30.9 18.3 %all-to-all-done.2 = bf16[512,2,1024]{2,0,1:T(8,128)(2,1)S(1)} async-done(((bf16[512,2,1024]{2,0,1:T(8,128)(2,1)}), bf16[512,2,1024]{2,0,1:T(8,128)(2,1)S(1)}, u32[]{:S(2)}, u32[]{:S(2)}) %all-to-all-start.2) | async-done | bytes 2097184 | tf_op jit(solution)/shard_map/all_to_all | solution.py:81
  50.5 5.6 %all-to-all-start.5 = ((bf16[512,2,2048]{2,0,1:T(8,128)(2,1)}), bf16[512,2,2048]{2,0,1:T(8,128)(2,1)}, u32[]{:S(2)}, u32[]{:S(2)}) async-start(bf16[512,2,2048]{2,0,1:T(8,128)(2,1)} %bitcast.110), calls=%async_computation.5 | async-start | bytes 8388608 | tf_op jit(solution)/shard_map/all_to_all | solution.py:82
  58.6 3.3 squeeze_reshape.12
  64.1 36.8 %all-to-all-done.5 = bf16[512,2,2048]{2,0,1:T(8,128)(2,1)} async-done(((bf16[512,2,2048]{2,0,1:T(8,128)(2,1)}), bf16[512,2,2048]{2,0,1:T(8,128)(2,1)}, u32[]{:S(2)}, u32[]{:S(2)}) %all-to-all-start.5) | async-done | bytes 4194336 | tf_op jit(solution)/shard_map/all_to_all | solution.py:82
  100.9 7.8 %squeeze_reshape.13 = bf16[1024,4,512]{2,1,0:T(4,128)(2,1)} reshape(bf16[2,512,2048]{2,1,0:T(8,128)(2,1)} %bitcast.21) | data formatting | bytes 8388608 | tf_op jit(solution)/shard_map/squeeze;reshape | solution.py:113
  108.7 7.5 %copy.65 = bf16[1024,4,512]{0,2,1:T(8,128)(2,1)} copy(bf16[1024,4,512]{2,1,0:T(4,128)(2,1)} %squeeze_reshape.13) | data formatting | bytes 8388608 | tf_op jit(solution)/shard_map/squeeze;reshape | solution.py:113
  116.3 5.7 %fusion.8 = f32[4,256,512]{2,1,0:T(8,128)} fusion(bf16[1024,4,512]{0,2,1:T(8,128)(2,1)} %copy.65, bf16[1024,4,256]{2,1,0:T(4,128)(2,1)} %multiply_convert_fusion.2), kind=kOutput, calls=%fused_computation.27 | convolution fusion | flops 1073741824 | bytes 8388608 | tf_op jit(solution)/shard_map/yij,yip->ijp/dot_general | solution.py:45
  123.6 3.8 all-to-all-start.1
  127.3 6.6 %copy.50 = bf16[512,4096]{0,1:T(8,128)(2,1)} copy(bf16[512,4096]{1,0:T(8,128)(2,1)} %param.14) | data formatting | bytes 8388608 | tf_op args[5]
  133.9 6.3 %copy.51 = bf16[512,2,2048]{2,0,1:T(8,128)(2,1)} copy(bf16[512,2,2048]{0,2,1:T(8,128)(2,1)} %bitcast.112) | data formatting | bytes 8388608 | tf_op jit(solution)/shard_map/all_to_all | solution.py:85
  140.3 8.6 %all-to-all-done.1 = bf16[512,2,1024]{2,0,1:T(8,128)(2,1)S(1)} async-done(((bf16[512,2,1024]{2,0,1:T(8,128)(2,1)}), bf16[512,2,1024]{2,0,1:T(8,128)(2,1)S(1)}, u32[]{:S(2)}, u32[]{:S(2)}) %all-to-all-start.1) | async-done | bytes 2097184 | tf_op jit(solution)/shard_map/all_to_all | solution.py:80
  148.8 5.6 %all-to-all-start = ((bf16[512,2,2048]{2,0,1:T(8,128)(2,1)}), bf16[512,2,2048]{2,0,1:T(8,128)(2,1)}, u32[]{:S(2)}, u32[]{:S(2)}) async-start(bf16[512,2,2048]{2,0,1:T(8,128)(2,1)} %copy.51), calls=%async_computation | async-start | bytes 8388608 | tf_op jit(solution)/shard_map/all_to_all | solution.py:85
  157.2 30.6 %all-reduce = f32[64]{0:T(128)S(1)} all-reduce(f32[64]{0:T(128)S(1)} %dynamic-update-slice), channel_id=2, replica_groups=mesh['seq'=16,'head'=2] {'seq'}, use_global_device_ids=true, to_apply=%add | all-reduce | flops 64 | bytes 512
  188.0 20.4 %all-gather.2 = f32[16,1,4]{2,1,0:T(1,128)S(1)} all-gather(f32[1,1,4]{2,1,0:T(1,128)S(1)} %get-tuple-element.113), channel_id=1, replica_groups=mesh['seq'=16,'head'=2] {'seq'}, dimensions={0}, use_global_device_ids=true | all-gather | bytes 272 | tf_op jit(solution)/shard_map/all_gather | solution.py:13
  208.5 5.2 %fusion.5 = f32[4,1024]{1,0:T(4,128)S(1)} fusion(f32[4,1024]{1,0:T(4,128)S(1)} %copy.58, f32[4,1024]{1,0:T(4,128)S(1)} %bitcast.123, pred[1024,1024]{1,0:T(8,128)(4,1)} %iota_compare_fusion), kind=kLoop, calls=%fused_computation.12 | loop fusion | flops 16773120 | bytes 1097728 | tf_op jit(solution)/shard_map/reduce_max | solution.py:64
  213.7 2.8 squeeze_reshape.11
  216.4 7.6 %add_divide_fusion = f32[512,2,2048]{2,0,1:T(8,128)} fusion(bf16[512,2,2048]{2,0,1:T(8,128)(2,1)} %all-to-all-done), kind=kLoop, calls=%fused_computation.17 | loop fusion | flops 8388608 | bytes 12582912 | tf_op jit(solution)/shard_map/div | solution.py:123
  224.0 9.3 %copy.68 = f32[1024,2048]{0,1:T(8,128)} copy(f32[1024,2048]{1,0:T(8,128)} %bitcast.109) | data formatting | bytes 16777216 | tf_op jit(solution)/shard_map/div | solution.py:123
  233.4 59.6 %all-gather.5.cloned.1.call-done = f32[64,256,512]{2,1,0:T(8,128)} async-done(((f32[4,256,512]{2,1,0:T(8,128)}), f32[64,256,512]{2,1,0:T(8,128)}) %all-gather.5.cloned.1.call-update) | async-done | bytes 33554448 | tf_op jit(solution)/shard_map/all_gather | solution.py:13
  293.2 40.0 %while.14 = (s32[]{:T(128)}, f32[4,256,512]{2,1,0:T(8,128)S(1)}, f32[4]{0:T(128)S(1)}, s32[]{:T(128)}, f32[16,4]{1,0:T(8,128)S(1)}, /*index=5*/f32[16,4]{1,0:T(8...) while((s32[]{:T(128)}, f32[4,256,512]{2,1,0:T(8,128)S(1)}, f32[4]{0:T(128)S(1)}, ...), condition=%wide.region_4.5_spmd, body=%wide.region_3.4_spmd.sunk | while | flops 1572885 | bytes 6291763 | solution.py:21
  293.3 2.6 fusion.26
  306.6 2.6 fusion.26
  333.3 14.9 %fusion.12 = f32[4,1024,512]{1,2,0:T(8,128)} fusion(bf16[1024,4,512]{0,2,1:T(8,128)(2,1)} %copy.65, f32[4,1024]{1,0:T(4,128)S(1)} %get-tuple-element.115, f32[4,1024]{1,0:T(4,128)S(1)} %copy.58, f32[4,1024]{1,0:T(4,128)S(1)} %bitcast.124, pred[1024,1024]{1,0:T(8,128)(4,1)S(1)} %copy-done.2, bf16[1024,4,256]{2,1,0:T(4,128)(2,1)} %copy-done, ...), kind=kOutput, calls=%fused_computation.30 | convolution fusion | flops 6467616768 | bytes 17874944 | tf_op jit(solution)/shard_map/hts,shv->thv/dot_general | solution.py:66
  348.2 6.2 %multiply_reduce_fusion = (f32[1024,4]{0,1:T(4,128)S(1)}, f32[1024,4,512]{0,2,1:T(8,128)S(1)}) fusion(bf16[1024,4,256]{2,1,0:T(4,128)(2,1)} %squeeze_reshape.11, f32[4,256,512]{2,1,0:T(8,128)S(1)} %get-tuple-element.65, f32[1024,4]{0,1:T(4,128)S(1)} %get-tuple-element.114, f32[4,1024,512]{1,2,0:T(8,128)} %fusion.12), kind=kOutput, calls=%fused_computation.19 | convolution fusion | flops 1082650624 | bytes 21004288 | tf_op jit(solution)/shard_map/ydw,dwl->ydl/dot_general | solution.py:69
  355.2 5.0 %fusion.6 = bf16[1024,2048]{0,1:T(8,128)(2,1)S(1)} fusion(f32[1024,2048]{0,1:T(8,128)} %copy.68, bf16[1024,4,512]{0,2,1:T(8,128)(2,1)S(1)} %multiply_convert_fusion.1), kind=kLoop, calls=%fused_computation.14 | loop fusion | flops 6291456 | bytes 16777216 | tf_op jit(solution)/shard_map/convert_element_type | solution.py:123
  361.0 49.4 %all_to_all.92 = bf16[2,512,2048]{1,2,0:T(8,128)(2,1)} all-to-all(bf16[2,512,2048]{1,2,0:T(8,128)(2,1)S(1)} %pad_maximum_fusion), channel_id=1, replica_groups=mesh['seq'=16,'head'=2] {'head'}, dimensions={0} | all-to-all | bytes 8388608 | tf_op jit(solution)/shard_map/all_to_all | solution.py:127
  410.4 6.3 %copy.72 = bf16[512,4096]{1,0:T(8,128)(2,1)} copy(bf16[512,4096]{0,1:T(8,128)(2,1)} %bitcast.111) | data formatting | bytes 8388608 | tf_op jit(solution)/shard_map/reshape | solution.py:126
  (93 shorter events, 52.2 us)
Async XLA Ops:
  7.8 5.9 %all-to-all-start.3 = ((bf16[512,2,4]{0,2,1:T(4,128)(2,1)}), bf16[512,2,4]{0,2,1:T(4,128)(2,1)S(1)}, u32[]{:S(2)}, u32[]{:S(2)}) async-start(bf16[512,2,4]{0,2,1:T(4,128)(2,1)} %all_to_all.77), calls=%async_computation.3 | async-start | bytes 16384 | tf_op jit(solution)/shard_map/all_to_all | solution.py:84
  13.7 8.6 %all-to-all-start.4 = ((bf16[512,2,4]{0,2,1:T(4,128)(2,1)}), bf16[512,2,4]{0,2,1:T(4,128)(2,1)S(1)}, u32[]{:S(2)}, u32[]{:S(2)}) async-start(bf16[512,2,4]{0,2,1:T(4,128)(2,1)} %all_to_all.79), calls=%async_computation.4 | async-start | bytes 16384 | tf_op jit(solution)/shard_map/all_to_all | solution.py:83
  22.3 26.9 %all-to-all-start.2 = ((bf16[512,2,1024]{2,0,1:T(8,128)(2,1)}), bf16[512,2,1024]{2,0,1:T(8,128)(2,1)S(1)}, u32[]{:S(2)}, u32[]{:S(2)}) async-start(bf16[512,2,1024]{2,0,1:T(8,128)(2,1)} %copy.54), calls=%async_computation.2 | async-start | bytes 4194304 | tf_op jit(solution)/shard_map/all_to_all | solution.py:81
  49.2 1.3 copy-start.1
  50.5 50.4 %all-to-all-start.5 = ((bf16[512,2,2048]{2,0,1:T(8,128)(2,1)}), bf16[512,2,2048]{2,0,1:T(8,128)(2,1)}, u32[]{:S(2)}, u32[]{:S(2)}) async-start(bf16[512,2,2048]{2,0,1:T(8,128)(2,1)} %bitcast.110), calls=%async_computation.5 | async-start | bytes 8388608 | tf_op jit(solution)/shard_map/all_to_all | solution.py:82
  56.1 236.8 %all-gather.5.cloned.1.call-start = ((), (), s32[]{:S(2)}) async-start(), calls=%async_computation.7 | async-start | bytes 35651584 | tf_op jit(solution)/shard_map/all_gather | solution.py:13
  61.9 46.9 %copy-start = (bf16[1024,4,256]{2,1,0:T(4,128)(2,1)}, bf16[1024,4,256]{2,1,0:T(4,128)(2,1)S(1)}, u32[]{:S(2)}) copy-start(bf16[1024,4,256]{2,1,0:T(4,128)(2,1)S(1)} %squeeze_reshape.12) | copy-start | bytes 6291460
  116.3 5.8 %copy-start.3 = (bf16[512,2048]{1,0:T(8,128)(2,1)S(1)}, bf16[512,2048]{1,0:T(8,128)(2,1)}, u32[]{:S(2)}) copy-start(bf16[512,2048]{1,0:T(8,128)(2,1)} %param.9) | copy-start | bytes 6291460
  123.6 25.2 %all-to-all-start.1 = ((bf16[512,2,1024]{2,0,1:T(8,128)(2,1)}), bf16[512,2,1024]{2,0,1:T(8,128)(2,1)S(1)}, u32[]{:S(2)}, u32[]{:S(2)}) async-start(bf16[512,2,1024]{2,0,1:T(8,128)(2,1)} %bitcast.115), calls=%async_computation.1 | async-start | bytes 4194304 | tf_op jit(solution)/shard_map/all_to_all | solution.py:80
  140.2 14.2 %copy-start.4 = (f32[2048]{0:T(1024)S(1)}, f32[2048]{0:T(1024)}, u32[]{:S(2)}) copy-start(f32[2048]{0:T(1024)} %param.15) | copy-start | bytes 24580
  140.2 14.2 %copy-start.5 = (u32[32]{0:T(128)S(1)}, u32[32]{0:T(128)}, u32[]{:S(2)}) copy-start(u32[32]{0:T(128)} %constant.48) | copy-start | bytes 388
  148.8 67.6 %all-to-all-start = ((bf16[512,2,2048]{2,0,1:T(8,128)(2,1)}), bf16[512,2,2048]{2,0,1:T(8,128)(2,1)}, u32[]{:S(2)}, u32[]{:S(2)}) async-start(bf16[512,2,2048]{2,0,1:T(8,128)(2,1)} %copy.51), calls=%async_computation | async-start | bytes 8388608 | tf_op jit(solution)/shard_map/all_to_all | solution.py:85
  293.2 40.1 %copy-start.2 = (pred[1024,1024]{1,0:T(8,128)(4,1)S(1)}, pred[1024,1024]{1,0:T(8,128)(4,1)}, u32[]{:S(2)}) copy-start(pred[1024,1024]{1,0:T(8,128)(4,1)} %iota_compare_fusion) | copy-start | bytes 3145732
Sparse Core Ops, SparseCore 0:
  122.1 170.7 all-gather.4
